TPU v7x, 128 devices: a whole 4x4x4 slice. The times are simulated.
128 devices in a mesh: sector: 64 (over y, z, x_hi, core), lift: 2 (over x_lo).
Axes of the slice: x: 4 (x_hi: 2, x_lo: 2; x = x_hi * 2 + x_lo), y: 4, z: 4, core: 2. Of those that a mesh axis runs over, the one named last changes fastest.
Arguments:
- right_side: float32 [128, 262144], P('lift', 'sector'), may hold values from -40 to 40
- diagonal: float32 [262144], P('sector'), may hold values from 1.9 to 2.6
- coupling: float32 [262144], P('sector'), may hold values from 0.3 to 0.94
- local_inverse: bfloat16 [256, 1024, 2048], P('sector'), may hold values from -0.1 to 0.6
- coarse_basis: bfloat16 [256, 16, 1024], P('sector'), may hold values from -0.1875 to 0.1875
- coarse_inverse: float32 [4096, 4096], P('sector', 'lift'), may hold values from -8 to 12
Outputs:
- solution: float32 [128, 262144], P('lift', 'sector')
- residual: float32 [128, 262144], P('lift', 'sector')
All inputs are finite; a program needn't handle non-finite values.
Results may differ from a plain program's by a relative error of at most 0.019.
Values may be sent and summed in bfloat16 or wider, within the bound.
No kernel may reach another device: no remote copies, remote signals or barrier semaphores. Data moves between devices by JAX's collectives and lax.ppermute only.
A program may use at most 128 MiB of HBM per device.

v0:
```python
import jax
import jax.numpy as jnp
from jax import lax
from jax.sharding import PartitionSpec as P

SWEEPS = 4
OUTER = 2


def extended_2(block, sides, width):
    for axis, dim in sides:
        count = lax.axis_size(axis)
        forward = [(i, i + 1) for i in range(count - 1)]
        forward.append((count - 1, 0))
        backward = [(target, source) for source, target in forward]
        low = lax.ppermute(
            lax.slice_in_dim(block, block.shape[dim] - width, None, axis=dim), axis, forward
        )
        high = lax.ppermute(lax.slice_in_dim(block, 0, width, axis=dim), axis, backward)
        block = jnp.concatenate([low, block, high], axis=dim)
    return block


def apply_op(extended, diag_part, link_part):
    return diag_part * extended[:, 1:-1] - link_part * (extended[:, :-2] + extended[:, 2:])


def body(right_side, diagonal, coupling, local_inverse, coarse_basis, coarse_inverse):
    highest = lax.Precision.HIGHEST
    num_cases, num_rows = right_side.shape
    sub_count = local_inverse.shape[0]
    own_rows = local_inverse.shape[1]
    inv_order = local_inverse.shape[2]
    margin = (inv_order - own_rows) // 2
    mode_count = coarse_basis.shape[1]
    basis_wide = coarse_basis.astype(jnp.float32)

    def rim_op(field):
        extended = extended_2(field, (("sector", 1),), 1)
        return apply_op(extended, diagonal, coupling)

    def intersection(half_res):
        return extended_2(half_res, (("sector", 1),), margin)

    def correct(padded):
        windows = jnp.stack(
            [
                padded[:, index * own_rows : index * own_rows + inv_order]
                for index in range(sub_count)
            ]
        )
        products = jnp.einsum(
            "jco,jko->cjk", windows, local_inverse, preferred_element_type=jnp.float32
        )
        return products.reshape(num_cases, num_rows)

    solution = jnp.zeros_like(right_side)
    residual = right_side
    for outer_step in range(OUTER):
        update = correct(intersection(residual.astype(jnp.bfloat16)))
        for sweep in range(SWEEPS - 1):
            padded = intersection((residual - rim_op(update)).astype(jnp.bfloat16))
            update = update + correct(padded)
        coarse_res = (residual - rim_op(update)).astype(jnp.bfloat16)
        projected = jnp.einsum(
            "cjk,jmk->cjm",
            coarse_res.reshape(num_cases, sub_count, own_rows),
            coarse_basis,
            preferred_element_type=jnp.float32,
        ).reshape(num_cases, sub_count * mode_count)
        gathered = lax.all_gather(projected, "sector", axis=1, tiled=True)
        swapped = lax.all_to_all(
            gathered.astype(jnp.bfloat16), "lift", split_axis=1, concat_axis=0, tiled=True
        ).astype(gathered.dtype)
        coarse_sol = lax.psum_scatter(
            jnp.dot(swapped, coarse_inverse.T, precision=highest).astype(jnp.bfloat16),
            "lift",
            scatter_dimension=0,
            tiled=True,
        ).astype(jnp.float32)
        coarse_wide = coarse_sol.reshape(num_cases, sub_count, mode_count)
        update = update + jnp.einsum(
            "cjm,jmk->cjk", coarse_wide, basis_wide, precision=highest
        ).reshape(num_cases, num_rows)
        image = rim_op(update)
        totals = lax.psum(
            (jnp.sum(residual * image, axis=1), jnp.sum(image * image, axis=1)), "sector"
        )
        alpha = totals[0] / (totals[1] + 1e-06)
        solution = solution + alpha[:, None] * update
        residual = residual - alpha[:, None] * image
    return (solution, residual)


def solution(mesh):
    in_specs = (
        P("lift", "sector"),
        P("sector"),
        P("sector"),
        P("sector", None, None),
        P("sector", None, None),
        P("sector", "lift"),
    )
    out_specs = (P("lift", "sector"), P("lift", "sector"))
    return jax.shard_map(body, mesh=mesh, in_specs=in_specs, out_specs=out_specs, check_vma=False)
```

profile of v0, /device:TPU:0, one launch (start us, length us, event | category | flops | bytes accessed | tf_op | source)
XLA Modules:
  0.0 904.0 jit_solution(17733858493407089266)
XLA Ops:
  8.7 8.6 collective-permute-start.1
  20.0 11.0 %convolution_bitcast_fusion.9 = f32[4,8,8,1024]{3,2,1,0:T(8,128)S(1)} fusion(bf16[4,1024,2048]{2,1,0:T(8,128)(2,1)} %param.9, bf16[1,64,2048]{2,1,0:T(8,128)(2,1)} %get-tuple-element.79, bf16[1,64,2048]{2,1,0:T(8,128)(2,1)S(1)} %get-tuple-element.77, bf16[1,64,2048]{2,1,0:T(8,128)(2,1)S(1)} %get-tuple-element.78, bf16[1,64,2048]{2,1,0:T(8,128)(2,1)S(1)} %get-tuple-element.76), kind=kOutput, calls=%fused_computation.9 | convolution fusion | flops 1075314688 | bytes 18874368 | tf_op jit(solution)/shard_map/jco,jko->cjk/dot_general | solution.py:52
  31.3 7.6 collective-permute-start.3
  41.3 7.5 collective-permute-start.5
  51.5 11.1 %convolution_bitcast_fusion.8 = f32[4,8,8,1024]{3,2,1,0:T(8,128)S(1)} fusion(bf16[4,1024,2048]{2,1,0:T(8,128)(2,1)} %param.9, bf16[1,64,2048]{2,1,0:T(8,128)(2,1)} %get-tuple-element.73, bf16[1,64,2048]{2,1,0:T(8,128)(2,1)S(1)} %get-tuple-element.71, bf16[1,64,2048]{2,1,0:T(8,128)(2,1)S(1)} %get-tuple-element.72, bf16[1,64,2048]{2,1,0:T(8,128)(2,1)S(1)} %get-tuple-element.70), kind=kOutput, calls=%fused_computation.8 | convolution fusion | flops 1075314688 | bytes 18874368 | tf_op jit(solution)/shard_map/jco,jko->cjk/dot_general | solution.py:52
  64.1 7.8 collective-permute-start.7
  74.3 7.5 collective-permute-start.9
  84.6 12.0 %convolution_bitcast_fusion.7 = f32[4,8,8,1024]{3,2,1,0:T(8,128)} fusion(bf16[4,1024,2048]{2,1,0:T(8,128)(2,1)} %param.9, bf16[1,64,2048]{2,1,0:T(8,128)(2,1)} %get-tuple-element.67, bf16[1,64,2048]{2,1,0:T(8,128)(2,1)S(1)} %get-tuple-element.65, bf16[1,64,2048]{2,1,0:T(8,128)(2,1)S(1)} %get-tuple-element.66, bf16[1,64,2048]{2,1,0:T(8,128)(2,1)S(1)} %get-tuple-element.64), kind=kOutput, calls=%fused_computation.7 | convolution fusion | flops 1075314688 | bytes 18874368 | tf_op jit(solution)/shard_map/jco,jko->cjk/dot_general | solution.py:52
  98.2 7.6 collective-permute-start.11
  108.1 7.5 collective-permute-start.13
  118.4 12.0 %convolution_bitcast_fusion.6 = f32[4,8,8,1024]{3,2,1,0:T(8,128)} fusion(bf16[4,1024,2048]{2,1,0:T(8,128)(2,1)} %param.9, bf16[1,64,2048]{2,1,0:T(8,128)(2,1)} %get-tuple-element.61, bf16[1,64,2048]{2,1,0:T(8,128)(2,1)S(1)} %get-tuple-element.59, bf16[1,64,2048]{2,1,0:T(8,128)(2,1)S(1)} %get-tuple-element.60, bf16[1,64,2048]{2,1,0:T(8,128)(2,1)S(1)} %get-tuple-element.58), kind=kOutput, calls=%fused_computation.6 | convolution fusion | flops 1075314688 | bytes 18874368 | tf_op jit(solution)/shard_map/jco,jko->cjk/dot_general | solution.py:52
  132.0 16.4 %collective-permute-start.15 = (f32[64,1]{1,0:T(8,128)S(1)}, f32[64,1]{1,0:T(8,128)S(1)}, u32[]{:S(2)}, u32[]{:S(2)}) collective-permute-start(f32[64,1]{1,0:T(8,128)S(1)} %get-tuple-element.27), channel_id=1, source_target_pairs={{2,0},{4,2},{6,4},{8,6},{10,8},{12,10},{14,12},{16,14},{18,16},{20... | collective-permute-start | bytes 776 | tf_op jit(solution)/shard_map/ppermute | solution.py:19
  151.8 92.6 %all_gather.6 = bf16[64,4096]{0,1:T(8,128)(2,1)S(1)} all-gather(bf16[64,64]{0,1:T(8,128)(2,1)S(1)} %bitcast.176), channel_id=1, replica_groups=mesh['sector'=64,'lift'=2] {'sector'}, dimensions={1}, use_global_device_ids=true | all-gather | bytes 532480 | tf_op jit(solution)/shard_map/all_gather | solution.py:71
  244.8 11.2 %all_to_all.38 = bf16[64,2,2048]{2,0,1:T(8,128)(2,1)S(1)} all-to-all(bf16[64,2,2048]{2,0,1:T(8,128)(2,1)S(1)} %bitcast.168), channel_id=1, replica_groups=mesh['sector'=64,'lift'=2] {'lift'}, dimensions={1} | all-to-all | bytes 1048576 | tf_op jit(solution)/shard_map/all_to_all | solution.py:72
  257.3 9.2 %reduce-scatter.3.cloned.1.call-done = bf16[64,64]{1,0:T(8,128)(2,1)} async-done(((bf16[128,64]{1,0:T(8,128)(2,1)}), bf16[64,64]{1,0:T(8,128)(2,1)}) %reduce-scatter.3.cloned.1.call-update) | async-done | bytes 8208 | tf_op jit(solution)/shard_map/reduce_scatter | solution.py:75
  270.0 7.5 collective-permute-start.17
  279.9 170.0 %all-reduce.1 = (f32[64]{0:T(128)S(1)}, f32[64]{0:T(128)S(1)}) all-reduce(f32[64]{0:T(128)S(1)} %get-tuple-element.5, f32[64]{0:T(128)S(1)} %get-tuple-element.4), channel_id=1, replica_groups=mesh['sector'=64,'lift'=2] {'sector'}, use_global_device_ids=true, to_apply=%region_2.0 | all-reduce | flops 128 | bytes 1024 | tf_op jit(solution)/shard_map/psum | solution.py:86
  462.1 11.9 %convolution_bitcast_fusion.4 = f32[4,8,8,1024]{3,2,1,0:T(8,128)} fusion(bf16[4,1024,2048]{2,1,0:T(8,128)(2,1)} %param.9, bf16[1,64,2048]{2,1,0:T(8,128)(2,1)S(1)} %get-tuple-element.55, bf16[1,64,2048]{2,1,0:T(8,128)(2,1)S(1)} %get-tuple-element.53, bf16[1,64,2048]{2,1,0:T(8,128)(2,1)S(1)} %get-tuple-element.54, bf16[1,64,2048]{2,1,0:T(8,128)(2,1)S(1)} %get-tuple-element.52), kind=kOutput, calls=%fused_computation.4 | convolution fusion | flops 1075314688 | bytes 18874368 | tf_op jit(solution)/shard_map/jco,jko->cjk/dot_general | solution.py:52
  475.5 7.5 collective-permute-start.21
  485.4 7.7 collective-permute-start.23
  495.9 12.1 %convolution_bitcast_fusion.3 = f32[4,8,8,1024]{3,2,1,0:T(8,128)} fusion(bf16[4,1024,2048]{2,1,0:T(8,128)(2,1)} %param.9, bf16[1,64,2048]{2,1,0:T(8,128)(2,1)} %get-tuple-element.49, bf16[1,64,2048]{2,1,0:T(8,128)(2,1)S(1)} %get-tuple-element.47, bf16[1,64,2048]{2,1,0:T(8,128)(2,1)S(1)} %get-tuple-element.48, bf16[1,64,2048]{2,1,0:T(8,128)(2,1)S(1)} %get-tuple-element.46), kind=kOutput, calls=%fused_computation.3 | convolution fusion | flops 1075314688 | bytes 18874368 | tf_op jit(solution)/shard_map/jco,jko->cjk/dot_general | solution.py:52
  510.7 7.6 collective-permute-start.25
  520.7 7.5 collective-permute-start.27
  530.9 12.0 %convolution_bitcast_fusion.2 = f32[4,8,8,1024]{3,2,1,0:T(8,128)} fusion(bf16[4,1024,2048]{2,1,0:T(8,128)(2,1)} %param.9, bf16[1,64,2048]{2,1,0:T(8,128)(2,1)} %get-tuple-element.43, bf16[1,64,2048]{2,1,0:T(8,128)(2,1)S(1)} %get-tuple-element.41, bf16[1,64,2048]{2,1,0:T(8,128)(2,1)S(1)} %get-tuple-element.42, bf16[1,64,2048]{2,1,0:T(8,128)(2,1)S(1)} %get-tuple-element.40), kind=kOutput, calls=%fused_computation.2 | convolution fusion | flops 1075314688 | bytes 18874368 | tf_op jit(solution)/shard_map/jco,jko->cjk/dot_general | solution.py:52
  544.5 7.6 collective-permute-start.29
  554.5 7.8 collective-permute-start.31
  564.3 12.0 %convolution_bitcast_fusion.1 = f32[4,8,8,1024]{3,2,1,0:T(8,128)} fusion(bf16[4,1024,2048]{2,1,0:T(8,128)(2,1)} %param.9, bf16[1,64,2048]{2,1,0:T(8,128)(2,1)S(1)} %get-tuple-element.37, bf16[1,64,2048]{2,1,0:T(8,128)(2,1)S(1)} %get-tuple-element.35, bf16[1,64,2048]{2,1,0:T(8,128)(2,1)S(1)} %get-tuple-element.36, bf16[1,64,2048]{2,1,0:T(8,128)(2,1)S(1)} %get-tuple-element.34), kind=kOutput, calls=%fused_computation.1 | convolution fusion | flops 1075314688 | bytes 18874368 | tf_op jit(solution)/shard_map/jco,jko->cjk/dot_general | solution.py:52
  579.2 7.6 collective-permute-start.33
  589.3 97.8 %all_gather.7 = bf16[64,4096]{0,1:T(8,128)(2,1)} all-gather(bf16[64,64]{0,1:T(8,128)(2,1)S(1)} %bitcast.177), channel_id=1, replica_groups=mesh['sector'=64,'lift'=2] {'sector'}, dimensions={1}, use_global_device_ids=true | all-gather | bytes 532480 | tf_op jit(solution)/shard_map/all_gather | solution.py:71
  688.7 11.2 %all_to_all.39 = bf16[64,2,2048]{2,0,1:T(8,128)(2,1)S(1)} all-to-all(bf16[64,2,2048]{2,0,1:T(8,128)(2,1)S(1)} %bitcast.170), channel_id=1, replica_groups=mesh['sector'=64,'lift'=2] {'lift'}, dimensions={1} | all-to-all | bytes 1048576 | tf_op jit(solution)/shard_map/all_to_all | solution.py:72
  701.1 9.2 %reduce-scatter.5.cloned.1.call-done = bf16[64,64]{1,0:T(8,128)(2,1)} async-done(((bf16[128,64]{1,0:T(8,128)(2,1)}), bf16[64,64]{1,0:T(8,128)(2,1)}) %reduce-scatter.5.cloned.1.call-update) | async-done | bytes 8208 | tf_op jit(solution)/shard_map/reduce_scatter | solution.py:75
  722.9 170.0 %all-reduce = (f32[64]{0:T(128)S(1)}, f32[64]{0:T(128)S(1)}) all-reduce(f32[64]{0:T(128)S(1)} %get-tuple-element.3, f32[64]{0:T(128)S(1)} %get-tuple-element.2), channel_id=1, replica_groups=mesh['sector'=64,'lift'=2] {'sector'}, use_global_device_ids=true, to_apply=%region_7.0 | all-reduce | flops 128 | bytes 1024 | tf_op jit(solution)/shard_map/psum | solution.py:86
  (161 shorter events, 92.2 us)
Async XLA Ops:
  7.2 259.2 %reduce-scatter.3.cloned.1.call-start = ((), (), s32[]{:S(2)}) async-start(), calls=%async_computation.4 | async-start | bytes 49152 | tf_op jit(solution)/shard_map/reduce_scatter | solution.py:75
  8.7 10.5 %collective-permute-start = (bf16[64,512]{1,0:T(8,128)(2,1)S(1)}, bf16[64,512]{1,0:T(8,128)(2,1)S(1)}, u32[]{:S(2)}, u32[]{:S(2)}) collective-permute-start(bf16[64,512]{1,0:T(8,128)(2,1)S(1)} %get-tuple-element.80), channel_id=1, source_target_pairs={{0,2},{2,4},{4,6},{6,8},{8,10},{10,12},{12,14},{14,16},{16,18},{18... | collective-permute-start | bytes 196616 | tf_op jit(solution)/shard_map/ppermute | solution.py:16
  8.7 10.5 %collective-permute-start.1 = (bf16[64,512]{1,0:T(8,128)(2,1)S(1)}, bf16[64,512]{1,0:T(8,128)(2,1)S(1)}, u32[]{:S(2)}, u32[]{:S(2)}) collective-permute-start(bf16[64,512]{1,0:T(8,128)(2,1)S(1)} %get-tuple-element.81), channel_id=1, source_target_pairs={{2,0},{4,2},{6,4},{8,6},{10,8},{12,10},{14,12},{16,14},{18,16},{20... | collective-permute-start | bytes 196616 | tf_op jit(solution)/shard_map/ppermute | solution.py:19
  31.3 9.1 %collective-permute-start.2 = (f32[64,1]{1,0:T(8,128)S(1)}, f32[64,1]{1,0:T(8,128)S(1)}, u32[]{:S(2)}, u32[]{:S(2)}) collective-permute-start(f32[64,1]{1,0:T(8,128)S(1)} %get-tuple-element.32), channel_id=1, source_target_pairs={{0,2},{2,4},{4,6},{6,8},{8,10},{10,12},{12,14},{14,16},{16,18},{18... | collective-permute-start | bytes 776 | tf_op jit(solution)/shard_map/ppermute | solution.py:16
  31.3 9.2 %collective-permute-start.3 = (f32[64,1]{1,0:T(8,128)S(1)}, f32[64,1]{1,0:T(8,128)S(1)}, u32[]{:S(2)}, u32[]{:S(2)}) collective-permute-start(f32[64,1]{1,0:T(8,128)S(1)} %get-tuple-element.33), channel_id=1, source_target_pairs={{2,0},{4,2},{6,4},{8,6},{10,8},{12,10},{14,12},{16,14},{18,16},{20... | collective-permute-start | bytes 776 | tf_op jit(solution)/shard_map/ppermute | solution.py:19
  41.2 9.5 %collective-permute-start.4 = (bf16[64,512]{1,0:T(8,128)(2,1)S(1)}, bf16[64,512]{1,0:T(8,128)(2,1)S(1)}, u32[]{:S(2)}, u32[]{:S(2)}) collective-permute-start(bf16[64,512]{1,0:T(8,128)(2,1)S(1)} %get-tuple-element.74), channel_id=1, source_target_pairs={{0,2},{2,4},{4,6},{6,8},{8,10},{10,12},{12,14},{14,16},{16,18},{18... | collective-permute-start | bytes 196616 | tf_op jit(solution)/shard_map/ppermute | solution.py:16
  41.3 9.4 %collective-permute-start.5 = (bf16[64,512]{1,0:T(8,128)(2,1)S(1)}, bf16[64,512]{1,0:T(8,128)(2,1)S(1)}, u32[]{:S(2)}, u32[]{:S(2)}) collective-permute-start(bf16[64,512]{1,0:T(8,128)(2,1)S(1)} %get-tuple-element.75), channel_id=1, source_target_pairs={{2,0},{4,2},{6,4},{8,6},{10,8},{12,10},{14,12},{16,14},{18,16},{20... | collective-permute-start | bytes 196616 | tf_op jit(solution)/shard_map/ppermute | solution.py:19
  64.1 9.1 %collective-permute-start.6 = (f32[64,1]{1,0:T(8,128)S(1)}, f32[64,1]{1,0:T(8,128)S(1)}, u32[]{:S(2)}, u32[]{:S(2)}) collective-permute-start(f32[64,1]{1,0:T(8,128)S(1)} %get-tuple-element.30), channel_id=1, source_target_pairs={{0,2},{2,4},{4,6},{6,8},{8,10},{10,12},{12,14},{14,16},{16,18},{18... | collective-permute-start | bytes 776 | tf_op jit(solution)/shard_map/ppermute | solution.py:16
  64.1 9.4 %collective-permute-start.7 = (f32[64,1]{1,0:T(8,128)S(1)}, f32[64,1]{1,0:T(8,128)S(1)}, u32[]{:S(2)}, u32[]{:S(2)}) collective-permute-start(f32[64,1]{1,0:T(8,128)S(1)} %get-tuple-element.31), channel_id=1, source_target_pairs={{2,0},{4,2},{6,4},{8,6},{10,8},{12,10},{14,12},{16,14},{18,16},{20... | collective-permute-start | bytes 776 | tf_op jit(solution)/shard_map/ppermute | solution.py:19
  74.3 9.5 %collective-permute-start.8 = (bf16[64,512]{1,0:T(8,128)(2,1)S(1)}, bf16[64,512]{1,0:T(8,128)(2,1)S(1)}, u32[]{:S(2)}, u32[]{:S(2)}) collective-permute-start(bf16[64,512]{1,0:T(8,128)(2,1)S(1)} %get-tuple-element.68), channel_id=1, source_target_pairs={{0,2},{2,4},{4,6},{6,8},{8,10},{10,12},{12,14},{14,16},{16,18},{18... | collective-permute-start | bytes 196616 | tf_op jit(solution)/shard_map/ppermute | solution.py:16
  74.3 9.4 %collective-permute-start.9 = (bf16[64,512]{1,0:T(8,128)(2,1)S(1)}, bf16[64,512]{1,0:T(8,128)(2,1)S(1)}, u32[]{:S(2)}, u32[]{:S(2)}) collective-permute-start(bf16[64,512]{1,0:T(8,128)(2,1)S(1)} %get-tuple-element.69), channel_id=1, source_target_pairs={{2,0},{4,2},{6,4},{8,6},{10,8},{12,10},{14,12},{16,14},{18,16},{20... | collective-permute-start | bytes 196616 | tf_op jit(solution)/shard_map/ppermute | solution.py:19
  98.1 9.1 %collective-permute-start.10 = (f32[64,1]{1,0:T(8,128)S(1)}, f32[64,1]{1,0:T(8,128)S(1)}, u32[]{:S(2)}, u32[]{:S(2)}) collective-permute-start(f32[64,1]{1,0:T(8,128)S(1)} %get-tuple-element.28), channel_id=1, source_target_pairs={{0,2},{2,4},{4,6},{6,8},{8,10},{10,12},{12,14},{14,16},{16,18},{18... | collective-permute-start | bytes 776 | tf_op jit(solution)/shard_map/ppermute | solution.py:16
  98.2 9.2 %collective-permute-start.11 = (f32[64,1]{1,0:T(8,128)S(1)}, f32[64,1]{1,0:T(8,128)S(1)}, u32[]{:S(2)}, u32[]{:S(2)}) collective-permute-start(f32[64,1]{1,0:T(8,128)S(1)} %get-tuple-element.29), channel_id=1, source_target_pairs={{2,0},{4,2},{6,4},{8,6},{10,8},{12,10},{14,12},{16,14},{18,16},{20... | collective-permute-start | bytes 776 | tf_op jit(solution)/shard_map/ppermute | solution.py:19
  108.1 9.5 %collective-permute-start.12 = (bf16[64,512]{1,0:T(8,128)(2,1)S(1)}, bf16[64,512]{1,0:T(8,128)(2,1)S(1)}, u32[]{:S(2)}, u32[]{:S(2)}) collective-permute-start(bf16[64,512]{1,0:T(8,128)(2,1)S(1)} %get-tuple-element.62), channel_id=1, source_target_pairs={{0,2},{2,4},{4,6},{6,8},{8,10},{10,12},{12,14},{14,16},{16,18},{18... | collective-permute-start | bytes 196616 | tf_op jit(solution)/shard_map/ppermute | solution.py:16
  108.1 9.4 %collective-permute-start.13 = (bf16[64,512]{1,0:T(8,128)(2,1)S(1)}, bf16[64,512]{1,0:T(8,128)(2,1)S(1)}, u32[]{:S(2)}, u32[]{:S(2)}) collective-permute-start(bf16[64,512]{1,0:T(8,128)(2,1)S(1)} %get-tuple-element.63), channel_id=1, source_target_pairs={{2,0},{4,2},{6,4},{8,6},{10,8},{12,10},{14,12},{16,14},{18,16},{20... | collective-permute-start | bytes 196616 | tf_op jit(solution)/shard_map/ppermute | solution.py:19
  132.0 16.4 %collective-permute-start.14 = (f32[64,1]{1,0:T(8,128)S(1)}, f32[64,1]{1,0:T(8,128)S(1)}, u32[]{:S(2)}, u32[]{:S(2)}) collective-permute-start(f32[64,1]{1,0:T(8,128)S(1)} %get-tuple-element.26), channel_id=1, source_target_pairs={{0,2},{2,4},{4,6},{6,8},{8,10},{10,12},{12,14},{14,16},{16,18},{18... | collective-permute-start | bytes 776 | tf_op jit(solution)/shard_map/ppermute | solution.py:16
  132.0 18.0 %collective-permute-start.15 = (f32[64,1]{1,0:T(8,128)S(1)}, f32[64,1]{1,0:T(8,128)S(1)}, u32[]{:S(2)}, u32[]{:S(2)}) collective-permute-start(f32[64,1]{1,0:T(8,128)S(1)} %get-tuple-element.27), channel_id=1, source_target_pairs={{2,0},{4,2},{6,4},{8,6},{10,8},{12,10},{14,12},{16,14},{18,16},{20... | collective-permute-start | bytes 776 | tf_op jit(solution)/shard_map/ppermute | solution.py:19
  257.2 453.1 %reduce-scatter.5.cloned.1.call-start = ((), (), s32[]{:S(2)}) async-start(), calls=%async_computation.5 | async-start | bytes 49152 | tf_op jit(solution)/shard_map/reduce_scatter | solution.py:75
  452.5 9.5 %collective-permute-start.18 = (bf16[64,512]{1,0:T(8,128)(2,1)S(1)}, bf16[64,512]{1,0:T(8,128)(2,1)S(1)}, u32[]{:S(2)}, u32[]{:S(2)}) collective-permute-start(bf16[64,512]{1,0:T(8,128)(2,1)S(1)} %get-tuple-element.56), channel_id=1, source_target_pairs={{0,2},{2,4},{4,6},{6,8},{8,10},{10,12},{12,14},{14,16},{16,18},{18... | collective-permute-start | bytes 196616 | tf_op jit(solution)/shard_map/ppermute | solution.py:16
  452.6 9.4 %collective-permute-start.19 = (bf16[64,512]{1,0:T(8,128)(2,1)S(1)}, bf16[64,512]{1,0:T(8,128)(2,1)S(1)}, u32[]{:S(2)}, u32[]{:S(2)}) collective-permute-start(bf16[64,512]{1,0:T(8,128)(2,1)S(1)} %get-tuple-element.57), channel_id=1, source_target_pairs={{2,0},{4,2},{6,4},{8,6},{10,8},{12,10},{14,12},{16,14},{18,16},{20... | collective-permute-start | bytes 196616 | tf_op jit(solution)/shard_map/ppermute | solution.py:19
  475.5 9.1 %collective-permute-start.21 = (f32[64,1]{1,0:T(8,128)S(1)}, f32[64,1]{1,0:T(8,128)S(1)}, u32[]{:S(2)}, u32[]{:S(2)}) collective-permute-start(f32[64,1]{1,0:T(8,128)S(1)} %get-tuple-element.23), channel_id=1, source_target_pairs={{2,0},{4,2},{6,4},{8,6},{10,8},{12,10},{14,12},{16,14},{18,16},{20... | collective-permute-start | bytes 776 | tf_op jit(solution)/shard_map/ppermute | solution.py:19
  485.3 9.5 %collective-permute-start.22 = (bf16[64,512]{1,0:T(8,128)(2,1)S(1)}, bf16[64,512]{1,0:T(8,128)(2,1)S(1)}, u32[]{:S(2)}, u32[]{:S(2)}) collective-permute-start(bf16[64,512]{1,0:T(8,128)(2,1)S(1)} %get-tuple-element.50), channel_id=1, source_target_pairs={{0,2},{2,4},{4,6},{6,8},{8,10},{10,12},{12,14},{14,16},{16,18},{18... | collective-permute-start | bytes 196616 | tf_op jit(solution)/shard_map/ppermute | solution.py:16
  485.4 9.7 %collective-permute-start.23 = (bf16[64,512]{1,0:T(8,128)(2,1)S(1)}, bf16[64,512]{1,0:T(8,128)(2,1)S(1)}, u32[]{:S(2)}, u32[]{:S(2)}) collective-permute-start(bf16[64,512]{1,0:T(8,128)(2,1)S(1)} %get-tuple-element.51), channel_id=1, source_target_pairs={{2,0},{4,2},{6,4},{8,6},{10,8},{12,10},{14,12},{16,14},{18,16},{20... | collective-permute-start | bytes 196616 | tf_op jit(solution)/shard_map/ppermute | solution.py:19
  510.7 9.1 %collective-permute-start.24 = (f32[64,1]{1,0:T(8,128)S(1)}, f32[64,1]{1,0:T(8,128)S(1)}, u32[]{:S(2)}, u32[]{:S(2)}) collective-permute-start(f32[64,1]{1,0:T(8,128)S(1)} %get-tuple-element.20), channel_id=1, source_target_pairs={{0,2},{2,4},{4,6},{6,8},{8,10},{10,12},{12,14},{14,16},{16,18},{18... | collective-permute-start | bytes 776 | tf_op jit(solution)/shard_map/ppermute | solution.py:16
  510.7 9.2 %collective-permute-start.25 = (f32[64,1]{1,0:T(8,128)S(1)}, f32[64,1]{1,0:T(8,128)S(1)}, u32[]{:S(2)}, u32[]{:S(2)}) collective-permute-start(f32[64,1]{1,0:T(8,128)S(1)} %get-tuple-element.21), channel_id=1, source_target_pairs={{2,0},{4,2},{6,4},{8,6},{10,8},{12,10},{14,12},{16,14},{18,16},{20... | collective-permute-start | bytes 776 | tf_op jit(solution)/shard_map/ppermute | solution.py:19
  520.6 9.5 %collective-permute-start.26 = (bf16[64,512]{1,0:T(8,128)(2,1)S(1)}, bf16[64,512]{1,0:T(8,128)(2,1)S(1)}, u32[]{:S(2)}, u32[]{:S(2)}) collective-permute-start(bf16[64,512]{1,0:T(8,128)(2,1)S(1)} %get-tuple-element.44), channel_id=1, source_target_pairs={{0,2},{2,4},{4,6},{6,8},{8,10},{10,12},{12,14},{14,16},{16,18},{18... | collective-permute-start | bytes 196616 | tf_op jit(solution)/shard_map/ppermute | solution.py:16
  520.7 9.4 %collective-permute-start.27 = (bf16[64,512]{1,0:T(8,128)(2,1)S(1)}, bf16[64,512]{1,0:T(8,128)(2,1)S(1)}, u32[]{:S(2)}, u32[]{:S(2)}) collective-permute-start(bf16[64,512]{1,0:T(8,128)(2,1)S(1)} %get-tuple-element.45), channel_id=1, source_target_pairs={{2,0},{4,2},{6,4},{8,6},{10,8},{12,10},{14,12},{16,14},{18,16},{20... | collective-permute-start | bytes 196616 | tf_op jit(solution)/shard_map/ppermute | solution.py:19
  544.5 9.2 %collective-permute-start.29 = (f32[64,1]{1,0:T(8,128)S(1)}, f32[64,1]{1,0:T(8,128)S(1)}, u32[]{:S(2)}, u32[]{:S(2)}) collective-permute-start(f32[64,1]{1,0:T(8,128)S(1)} %get-tuple-element.19), channel_id=1, source_target_pairs={{2,0},{4,2},{6,4},{8,6},{10,8},{12,10},{14,12},{16,14},{18,16},{20... | collective-permute-start | bytes 776 | tf_op jit(solution)/shard_map/ppermute | solution.py:19
  554.4 9.5 %collective-permute-start.30 = (bf16[64,512]{1,0:T(8,128)(2,1)S(1)}, bf16[64,512]{1,0:T(8,128)(2,1)S(1)}, u32[]{:S(2)}, u32[]{:S(2)}) collective-permute-start(bf16[64,512]{1,0:T(8,128)(2,1)S(1)} %get-tuple-element.38), channel_id=1, source_target_pairs={{0,2},{2,4},{4,6},{6,8},{8,10},{10,12},{12,14},{14,16},{16,18},{18... | collective-permute-start | bytes 196616 | tf_op jit(solution)/shard_map/ppermute | solution.py:16
  554.5 9.7 %collective-permute-start.31 = (bf16[64,512]{1,0:T(8,128)(2,1)S(1)}, bf16[64,512]{1,0:T(8,128)(2,1)S(1)}, u32[]{:S(2)}, u32[]{:S(2)}) collective-permute-start(bf16[64,512]{1,0:T(8,128)(2,1)S(1)} %get-tuple-element.39), channel_id=1, source_target_pairs={{2,0},{4,2},{6,4},{8,6},{10,8},{12,10},{14,12},{16,14},{18,16},{20... | collective-permute-start | bytes 196616 | tf_op jit(solution)/shard_map/ppermute | solution.py:19
  579.1 9.1 %collective-permute-start.32 = (f32[64,1]{1,0:T(8,128)S(1)}, f32[64,1]{1,0:T(8,128)S(1)}, u32[]{:S(2)}, u32[]{:S(2)}) collective-permute-start(f32[64,1]{1,0:T(8,128)S(1)} %get-tuple-element.16), channel_id=1, source_target_pairs={{0,2},{2,4},{4,6},{6,8},{8,10},{10,12},{12,14},{14,16},{16,18},{18... | collective-permute-start | bytes 776 | tf_op jit(solution)/shard_map/ppermute | solution.py:16
  579.2 9.2 %collective-permute-start.33 = (f32[64,1]{1,0:T(8,128)S(1)}, f32[64,1]{1,0:T(8,128)S(1)}, u32[]{:S(2)}, u32[]{:S(2)}) collective-permute-start(f32[64,1]{1,0:T(8,128)S(1)} %get-tuple-element.17), channel_id=1, source_target_pairs={{2,0},{4,2},{6,4},{8,6},{10,8},{12,10},{14,12},{16,14},{18,16},{20... | collective-permute-start | bytes 776 | tf_op jit(solution)/shard_map/ppermute | solution.py:19
  (21 other events, 875.6 us)
Sparse Core Ops, SparseCore 0:
  257.3 9.0 reduce-scatter.2
  701.2 9.0 reduce-scatter.4
where the time goes:
time: 913 us; the launch traced here: 904 us
  blocking collectives  553 us (61%)
  starting transfers between devices  147 us (16%)
  matrix products  99.6 us (11%)
  waiting for transfers between devices  49.7 us (5%)
  other arithmetic  27.1 us (3%)
  between operations  15.1 us (2%)
  local copies, waits for them, and re-layouts  12.7 us (1%)
    psum x2, blocking collectives, body(): lax.psum((jnp.sum(residual * image, axis=1), jnp.sum(image * image, axis=...  340 us
    all_gather x2, blocking collectives, body(): gathered = lax.all_gather(projected, 'sector', axis=1, tiled=True)  190 us
    ppermute x18, starting transfers between devices, extended_2(): lax.ppermute(lax.slice_in_dim(block, 0, width, axis=dim), axis, backward)  146 us
    dot_general x8, matrix products, correct(): jnp.einsum('jco,jko->cjk', windows, local_inverse, preferred_element_type...  94.2 us
    ppermute x18, waiting for transfers between devices, extended_2(): lax.ppermute(lax.slice_in_dim(block, block.shape[dim] - width, None, axis...  28.2 us
    all_to_all x2, blocking collectives, body(): lax.all_to_all(gathered.astype(jnp.bfloat16), 'lift', split_axis=1, conca...  22.3 us
    reduce_scatter x2, waiting for transfers between devices, body(): lax.psum_scatter(jnp.dot(swapped, coarse_inverse.T, precision=highest).as...  18.4 us
  transfers between devices with their start and end apart: 38, of which 29 were waited for; matrix products, arithmetic and copies ran while one was open for 0% of the time, Pallas kernels for 0%

commit v1 on v0

--- a/solution.py
+++ b/solution.py
@@ -68,7 +68,9 @@
             coarse_basis,
             preferred_element_type=jnp.float32,
         ).reshape(num_cases, sub_count * mode_count)
-        gathered = lax.all_gather(projected, "sector", axis=1, tiled=True)
+        gathered = jnp.concatenate(
+            lax.all_to_all(jnp.stack([projected] * lax.axis_size("sector")), "sector", 0, 0), axis=1
+        )
         swapped = lax.all_to_all(
             gathered.astype(jnp.bfloat16), "lift", split_axis=1, concat_axis=0, tiled=True
         ).astype(gathered.dtype)

time: 913 us -> 778 us (0.85)
  blocking collectives: 553 us -> 410 us
  local copies, waits for them, and re-layouts: 12.7 us -> 33.8 us
    all_gather x2 -> x0, blocking collectives: 190 us -> none  [body(): gathered = lax.all_gather(projected, 'sector', axis=1, tiled=True)]
    all_to_all x0 -> x2, blocking collectives: none -> 47.9 us  [body(): lax.all_to_all(jnp.stack([projected] * lax.axis_size('sector')), 'sector'...]
    convert_element_type x0 -> x6, local copies, waits for them, and re-layouts: none -> 10.8 us  [body(): gathered.astype(jnp.bfloat16)]
    unnamed x30 -> x32, local copies, waits for them, and re-layouts: 0.09 us -> 10.8 us
  transfers between devices with their start and end apart: 38 -> 38, of which waited for: 29 -> 30; matrix products, arithmetic and copies ran while one was open for 0% -> 0% of each run, Pallas kernels for 0% -> 0%
where the time goes in v1:
time: 778 us; the launch traced here: 769 us
  blocking collectives  410 us (53%)
  starting transfers between devices  139 us (18%)
  matrix products  97.7 us (13%)
  waiting for transfers between devices  46.4 us (6%)
  local copies, waits for them, and re-layouts  33.8 us (4%)
  other arithmetic  27.1 us (3%)
  between operations  15.1 us (2%)
    psum x2, blocking collectives, body(): lax.psum((jnp.sum(residual * image, axis=1), jnp.sum(image * image, axis=...  340 us
    ppermute x18, starting transfers between devices, extended_2(): lax.ppermute(lax.slice_in_dim(block, 0, width, axis=dim), axis, backward)  138 us
    dot_general x8, matrix products, correct(): jnp.einsum('jco,jko->cjk', windows, local_inverse, preferred_element_type...  93.2 us
    all_to_all x2, blocking collectives, body(): lax.all_to_all(jnp.stack([projected] * lax.axis_size('sector')), 'sector'...  47.9 us
    ppermute x18, waiting for transfers between devices, extended_2(): lax.ppermute(lax.slice_in_dim(block, block.shape[dim] - width, None, axis...  29.2 us
    all_to_all x2, blocking collectives, body(): lax.all_to_all(gathered.astype(jnp.bfloat16), 'lift', split_axis=1, conca...  21.7 us
  transfers between devices with their start and end apart: 38, of which 30 were waited for; matrix products, arithmetic and copies ran while one was open for 0% of the time, Pallas kernels for 0%

profile of v1, /device:TPU:0, one launch (start us, length us, event | category | flops | bytes accessed | tf_op | source)
XLA Modules:
  0.0 768.5 jit_solution(11535195378229328090)
XLA Ops:
  8.7 8.6 %collective-permute-start.1 = (bf16[64,512]{1,0:T(8,128)(2,1)S(1)}, bf16[64,512]{1,0:T(8,128)(2,1)S(1)}, u32[]{:S(2)}, u32[]{:S(2)}) collective-permute-start(bf16[64,512]{1,0:T(8,128)(2,1)S(1)} %get-tuple-element.81), channel_id=1, source_target_pairs={{2,0},{4,2},{6,4},{8,6},{10,8},{12,10},{14,12},{16,14},{18,16},{20... | collective-permute-start | bytes 196616 | tf_op jit(solution)/shard_map/ppermute | solution.py:19
  20.0 11.0 %convolution_bitcast_fusion.9 = f32[4,8,8,1024]{3,2,1,0:T(8,128)S(1)} fusion(bf16[4,1024,2048]{2,1,0:T(8,128)(2,1)} %param.9, bf16[1,64,2048]{2,1,0:T(8,128)(2,1)} %get-tuple-element.79, bf16[1,64,2048]{2,1,0:T(8,128)(2,1)S(1)} %get-tuple-element.77, bf16[1,64,2048]{2,1,0:T(8,128)(2,1)S(1)} %get-tuple-element.78, bf16[1,64,2048]{2,1,0:T(8,128)(2,1)S(1)} %get-tuple-element.76), kind=kOutput, calls=%fused_computation.9 | convolution fusion | flops 1075314688 | bytes 18874368 | tf_op jit(solution)/shard_map/jco,jko->cjk/dot_general | solution.py:52
  31.3 7.6 collective-permute-start.3
  41.3 7.5 collective-permute-start.5
  51.5 11.1 %convolution_bitcast_fusion.8 = f32[4,8,8,1024]{3,2,1,0:T(8,128)S(1)} fusion(bf16[4,1024,2048]{2,1,0:T(8,128)(2,1)} %param.9, bf16[1,64,2048]{2,1,0:T(8,128)(2,1)} %get-tuple-element.73, bf16[1,64,2048]{2,1,0:T(8,128)(2,1)S(1)} %get-tuple-element.71, bf16[1,64,2048]{2,1,0:T(8,128)(2,1)S(1)} %get-tuple-element.72, bf16[1,64,2048]{2,1,0:T(8,128)(2,1)S(1)} %get-tuple-element.70), kind=kOutput, calls=%fused_computation.8 | convolution fusion | flops 1075314688 | bytes 18874368 | tf_op jit(solution)/shard_map/jco,jko->cjk/dot_general | solution.py:52
  64.1 7.8 %collective-permute-start.7 = (f32[64,1]{1,0:T(8,128)S(1)}, f32[64,1]{1,0:T(8,128)S(1)}, u32[]{:S(2)}, u32[]{:S(2)}) collective-permute-start(f32[64,1]{1,0:T(8,128)S(1)} %get-tuple-element.31), channel_id=1, source_target_pairs={{2,0},{4,2},{6,4},{8,6},{10,8},{12,10},{14,12},{16,14},{18,16},{20... | collective-permute-start | bytes 776 | tf_op jit(solution)/shard_map/ppermute | solution.py:19
  74.3 7.5 collective-permute-start.9
  84.6 12.0 %convolution_bitcast_fusion.7 = f32[4,8,8,1024]{3,2,1,0:T(8,128)} fusion(bf16[4,1024,2048]{2,1,0:T(8,128)(2,1)} %param.9, bf16[1,64,2048]{2,1,0:T(8,128)(2,1)} %get-tuple-element.67, bf16[1,64,2048]{2,1,0:T(8,128)(2,1)S(1)} %get-tuple-element.65, bf16[1,64,2048]{2,1,0:T(8,128)(2,1)S(1)} %get-tuple-element.66, bf16[1,64,2048]{2,1,0:T(8,128)(2,1)S(1)} %get-tuple-element.64), kind=kOutput, calls=%fused_computation.7 | convolution fusion | flops 1075314688 | bytes 18874368 | tf_op jit(solution)/shard_map/jco,jko->cjk/dot_general | solution.py:52
  98.1 7.6 collective-permute-start.11
  108.1 7.5 collective-permute-start.13
  118.4 11.0 %convolution_bitcast_fusion.6 = f32[4,8,8,1024]{3,2,1,0:T(8,128)S(1)} fusion(bf16[4,1024,2048]{2,1,0:T(8,128)(2,1)} %param.9, bf16[1,64,2048]{2,1,0:T(8,128)(2,1)} %get-tuple-element.61, bf16[1,64,2048]{2,1,0:T(8,128)(2,1)S(1)} %get-tuple-element.59, bf16[1,64,2048]{2,1,0:T(8,128)(2,1)S(1)} %get-tuple-element.60, bf16[1,64,2048]{2,1,0:T(8,128)(2,1)S(1)} %get-tuple-element.58), kind=kOutput, calls=%fused_computation.6 | convolution fusion | flops 1075314688 | bytes 18874368 | tf_op jit(solution)/shard_map/jco,jko->cjk/dot_general | solution.py:52
  131.0 8.0 %collective-permute-start.15 = (f32[64,1]{1,0:T(8,128)S(1)}, f32[64,1]{1,0:T(8,128)S(1)}, u32[]{:S(2)}, u32[]{:S(2)}) collective-permute-start(f32[64,1]{1,0:T(8,128)S(1)} %get-tuple-element.27), channel_id=1, source_target_pairs={{2,0},{4,2},{6,4},{8,6},{10,8},{12,10},{14,12},{16,14},{18,16},{20... | collective-permute-start | bytes 776 | tf_op jit(solution)/shard_map/ppermute | solution.py:19
  146.1 23.9 %all_to_all.42 = bf16[64,2,2048]{2,1,0:T(2,128)(2,1)} all-to-all(bf16[64,2,2048]{2,1,0:T(2,128)(2,1)S(1)} %reshape.82), channel_id=1, replica_groups=mesh['sector'=64,'lift'=2] {'sector'}, dimensions={0} | all-to-all | bytes 1048576 | tf_op jit(solution)/shard_map/all_to_all | solution.py:72
  178.4 10.9 %all_to_all.43 = bf16[64,2,2048]{2,0,1:T(8,128)(2,1)S(1)} all-to-all(bf16[64,2,2048]{2,0,1:T(8,128)(2,1)S(1)} %copy.48), channel_id=1, replica_groups=mesh['sector'=64,'lift'=2] {'lift'}, dimensions={1} | all-to-all | bytes 1048576 | tf_op jit(solution)/shard_map/all_to_all | solution.py:74
  190.6 7.6 reduce-scatter.3.cloned.1.call-done
  209.5 170.0 %all-reduce.1 = (f32[64]{0:T(128)S(1)}, f32[64]{0:T(128)S(1)}) all-reduce(f32[64]{0:T(128)S(1)} %get-tuple-element.5, f32[64]{0:T(128)S(1)} %get-tuple-element.4), channel_id=1, replica_groups=mesh['sector'=64,'lift'=2] {'sector'}, use_global_device_ids=true, to_apply=%region_2.0 | all-reduce | flops 128 | bytes 1024 | tf_op jit(solution)/shard_map/psum | solution.py:88
  382.1 7.6 collective-permute-start.19
  391.8 11.9 %convolution_bitcast_fusion.4 = f32[4,8,8,1024]{3,2,1,0:T(8,128)} fusion(bf16[4,1024,2048]{2,1,0:T(8,128)(2,1)} %param.9, bf16[1,64,2048]{2,1,0:T(8,128)(2,1)S(1)} %get-tuple-element.55, bf16[1,64,2048]{2,1,0:T(8,128)(2,1)S(1)} %get-tuple-element.53, bf16[1,64,2048]{2,1,0:T(8,128)(2,1)S(1)} %get-tuple-element.54, bf16[1,64,2048]{2,1,0:T(8,128)(2,1)S(1)} %get-tuple-element.52), kind=kOutput, calls=%fused_computation.4 | convolution fusion | flops 1075314688 | bytes 18874368 | tf_op jit(solution)/shard_map/jco,jko->cjk/dot_general | solution.py:52
  405.1 7.6 collective-permute-start.21
  415.1 7.5 collective-permute-start.23
  425.4 12.1 %convolution_bitcast_fusion.3 = f32[4,8,8,1024]{3,2,1,0:T(8,128)} fusion(bf16[4,1024,2048]{2,1,0:T(8,128)(2,1)} %param.9, bf16[1,64,2048]{2,1,0:T(8,128)(2,1)} %get-tuple-element.49, bf16[1,64,2048]{2,1,0:T(8,128)(2,1)S(1)} %get-tuple-element.47, bf16[1,64,2048]{2,1,0:T(8,128)(2,1)S(1)} %get-tuple-element.48, bf16[1,64,2048]{2,1,0:T(8,128)(2,1)S(1)} %get-tuple-element.46), kind=kOutput, calls=%fused_computation.3 | convolution fusion | flops 1075314688 | bytes 18874368 | tf_op jit(solution)/shard_map/jco,jko->cjk/dot_general | solution.py:52
  440.2 7.6 collective-permute-start.25
  450.2 7.7 %collective-permute-start.27 = (bf16[64,512]{1,0:T(8,128)(2,1)S(1)}, bf16[64,512]{1,0:T(8,128)(2,1)S(1)}, u32[]{:S(2)}, u32[]{:S(2)}) collective-permute-start(bf16[64,512]{1,0:T(8,128)(2,1)S(1)} %get-tuple-element.45), channel_id=1, source_target_pairs={{2,0},{4,2},{6,4},{8,6},{10,8},{12,10},{14,12},{16,14},{18,16},{20... | collective-permute-start | bytes 196616 | tf_op jit(solution)/shard_map/ppermute | solution.py:19
  460.6 12.0 %convolution_bitcast_fusion.2 = f32[4,8,8,1024]{3,2,1,0:T(8,128)} fusion(bf16[4,1024,2048]{2,1,0:T(8,128)(2,1)} %param.9, bf16[1,64,2048]{2,1,0:T(8,128)(2,1)} %get-tuple-element.43, bf16[1,64,2048]{2,1,0:T(8,128)(2,1)S(1)} %get-tuple-element.41, bf16[1,64,2048]{2,1,0:T(8,128)(2,1)S(1)} %get-tuple-element.42, bf16[1,64,2048]{2,1,0:T(8,128)(2,1)S(1)} %get-tuple-element.40), kind=kOutput, calls=%fused_computation.2 | convolution fusion | flops 1075314688 | bytes 18874368 | tf_op jit(solution)/shard_map/jco,jko->cjk/dot_general | solution.py:52
  474.2 7.6 collective-permute-start.29
  484.2 7.5 collective-permute-start.31
  493.7 12.0 %convolution_bitcast_fusion.1 = f32[4,8,8,1024]{3,2,1,0:T(8,128)} fusion(bf16[4,1024,2048]{2,1,0:T(8,128)(2,1)} %param.9, bf16[1,64,2048]{2,1,0:T(8,128)(2,1)S(1)} %get-tuple-element.37, bf16[1,64,2048]{2,1,0:T(8,128)(2,1)S(1)} %get-tuple-element.35, bf16[1,64,2048]{2,1,0:T(8,128)(2,1)S(1)} %get-tuple-element.36, bf16[1,64,2048]{2,1,0:T(8,128)(2,1)S(1)} %get-tuple-element.34), kind=kOutput, calls=%fused_computation.1 | convolution fusion | flops 1075314688 | bytes 18874368 | tf_op jit(solution)/shard_map/jco,jko->cjk/dot_general | solution.py:52
  508.6 7.8 %collective-permute-start.33 = (f32[64,1]{1,0:T(8,128)S(1)}, f32[64,1]{1,0:T(8,128)S(1)}, u32[]{:S(2)}, u32[]{:S(2)}) collective-permute-start(f32[64,1]{1,0:T(8,128)S(1)} %get-tuple-element.17), channel_id=1, source_target_pairs={{2,0},{4,2},{6,4},{8,6},{10,8},{12,10},{14,12},{16,14},{18,16},{20... | collective-permute-start | bytes 776 | tf_op jit(solution)/shard_map/ppermute | solution.py:19
  522.7 23.9 %all_to_all.44 = bf16[64,2,2048]{2,1,0:T(2,128)(2,1)} all-to-all(bf16[64,2,2048]{2,1,0:T(2,128)(2,1)S(1)} %reshape.84), channel_id=1, replica_groups=mesh['sector'=64,'lift'=2] {'sector'}, dimensions={0} | all-to-all | bytes 1048576 | tf_op jit(solution)/shard_map/all_to_all | solution.py:72
  555.1 10.9 %all_to_all.45 = bf16[64,2,2048]{2,0,1:T(8,128)(2,1)S(1)} all-to-all(bf16[64,2,2048]{2,0,1:T(8,128)(2,1)S(1)} %copy.58), channel_id=1, replica_groups=mesh['sector'=64,'lift'=2] {'lift'}, dimensions={1} | all-to-all | bytes 1048576 | tf_op jit(solution)/shard_map/all_to_all | solution.py:74
  567.2 7.6 reduce-scatter.5.cloned.1.call-done
  587.4 170.0 %all-reduce = (f32[64]{0:T(128)S(1)}, f32[64]{0:T(128)S(1)}) all-reduce(f32[64]{0:T(128)S(1)} %get-tuple-element.3, f32[64]{0:T(128)S(1)} %get-tuple-element.2), channel_id=1, replica_groups=mesh['sector'=64,'lift'=2] {'sector'}, use_global_device_ids=true, to_apply=%region_7.0 | all-reduce | flops 128 | bytes 1024 | tf_op jit(solution)/shard_map/psum | solution.py:88
  (169 shorter events, 112.4 us)
Async XLA Ops:
  7.2 190.9 %reduce-scatter.3.cloned.1.call-start = ((), (), s32[]{:S(2)}) async-start(), calls=%async_computation.6 | async-start | bytes 49152 | tf_op jit(solution)/shard_map/reduce_scatter | solution.py:77
  8.7 10.5 %collective-permute-start = (bf16[64,512]{1,0:T(8,128)(2,1)S(1)}, bf16[64,512]{1,0:T(8,128)(2,1)S(1)}, u32[]{:S(2)}, u32[]{:S(2)}) collective-permute-start(bf16[64,512]{1,0:T(8,128)(2,1)S(1)} %get-tuple-element.80), channel_id=1, source_target_pairs={{0,2},{2,4},{4,6},{6,8},{8,10},{10,12},{12,14},{14,16},{16,18},{18... | collective-permute-start | bytes 196616 | tf_op jit(solution)/shard_map/ppermute | solution.py:16
  8.7 10.5 %collective-permute-start.1 = (bf16[64,512]{1,0:T(8,128)(2,1)S(1)}, bf16[64,512]{1,0:T(8,128)(2,1)S(1)}, u32[]{:S(2)}, u32[]{:S(2)}) collective-permute-start(bf16[64,512]{1,0:T(8,128)(2,1)S(1)} %get-tuple-element.81), channel_id=1, source_target_pairs={{2,0},{4,2},{6,4},{8,6},{10,8},{12,10},{14,12},{16,14},{18,16},{20... | collective-permute-start | bytes 196616 | tf_op jit(solution)/shard_map/ppermute | solution.py:19
  31.3 9.1 %collective-permute-start.2 = (f32[64,1]{1,0:T(8,128)S(1)}, f32[64,1]{1,0:T(8,128)S(1)}, u32[]{:S(2)}, u32[]{:S(2)}) collective-permute-start(f32[64,1]{1,0:T(8,128)S(1)} %get-tuple-element.32), channel_id=1, source_target_pairs={{0,2},{2,4},{4,6},{6,8},{8,10},{10,12},{12,14},{14,16},{16,18},{18... | collective-permute-start | bytes 776 | tf_op jit(solution)/shard_map/ppermute | solution.py:16
  31.3 9.2 %collective-permute-start.3 = (f32[64,1]{1,0:T(8,128)S(1)}, f32[64,1]{1,0:T(8,128)S(1)}, u32[]{:S(2)}, u32[]{:S(2)}) collective-permute-start(f32[64,1]{1,0:T(8,128)S(1)} %get-tuple-element.33), channel_id=1, source_target_pairs={{2,0},{4,2},{6,4},{8,6},{10,8},{12,10},{14,12},{16,14},{18,16},{20... | collective-permute-start | bytes 776 | tf_op jit(solution)/shard_map/ppermute | solution.py:19
  41.2 9.5 %collective-permute-start.4 = (bf16[64,512]{1,0:T(8,128)(2,1)S(1)}, bf16[64,512]{1,0:T(8,128)(2,1)S(1)}, u32[]{:S(2)}, u32[]{:S(2)}) collective-permute-start(bf16[64,512]{1,0:T(8,128)(2,1)S(1)} %get-tuple-element.74), channel_id=1, source_target_pairs={{0,2},{2,4},{4,6},{6,8},{8,10},{10,12},{12,14},{14,16},{16,18},{18... | collective-permute-start | bytes 196616 | tf_op jit(solution)/shard_map/ppermute | solution.py:16
  41.3 9.4 %collective-permute-start.5 = (bf16[64,512]{1,0:T(8,128)(2,1)S(1)}, bf16[64,512]{1,0:T(8,128)(2,1)S(1)}, u32[]{:S(2)}, u32[]{:S(2)}) collective-permute-start(bf16[64,512]{1,0:T(8,128)(2,1)S(1)} %get-tuple-element.75), channel_id=1, source_target_pairs={{2,0},{4,2},{6,4},{8,6},{10,8},{12,10},{14,12},{16,14},{18,16},{20... | collective-permute-start | bytes 196616 | tf_op jit(solution)/shard_map/ppermute | solution.py:19
  64.1 9.1 %collective-permute-start.6 = (f32[64,1]{1,0:T(8,128)S(1)}, f32[64,1]{1,0:T(8,128)S(1)}, u32[]{:S(2)}, u32[]{:S(2)}) collective-permute-start(f32[64,1]{1,0:T(8,128)S(1)} %get-tuple-element.30), channel_id=1, source_target_pairs={{0,2},{2,4},{4,6},{6,8},{8,10},{10,12},{12,14},{14,16},{16,18},{18... | collective-permute-start | bytes 776 | tf_op jit(solution)/shard_map/ppermute | solution.py:16
  64.1 9.4 %collective-permute-start.7 = (f32[64,1]{1,0:T(8,128)S(1)}, f32[64,1]{1,0:T(8,128)S(1)}, u32[]{:S(2)}, u32[]{:S(2)}) collective-permute-start(f32[64,1]{1,0:T(8,128)S(1)} %get-tuple-element.31), channel_id=1, source_target_pairs={{2,0},{4,2},{6,4},{8,6},{10,8},{12,10},{14,12},{16,14},{18,16},{20... | collective-permute-start | bytes 776 | tf_op jit(solution)/shard_map/ppermute | solution.py:19
  74.2 9.5 %collective-permute-start.8 = (bf16[64,512]{1,0:T(8,128)(2,1)S(1)}, bf16[64,512]{1,0:T(8,128)(2,1)S(1)}, u32[]{:S(2)}, u32[]{:S(2)}) collective-permute-start(bf16[64,512]{1,0:T(8,128)(2,1)S(1)} %get-tuple-element.68), channel_id=1, source_target_pairs={{0,2},{2,4},{4,6},{6,8},{8,10},{10,12},{12,14},{14,16},{16,18},{18... | collective-permute-start | bytes 196616 | tf_op jit(solution)/shard_map/ppermute | solution.py:16
  74.3 9.4 %collective-permute-start.9 = (bf16[64,512]{1,0:T(8,128)(2,1)S(1)}, bf16[64,512]{1,0:T(8,128)(2,1)S(1)}, u32[]{:S(2)}, u32[]{:S(2)}) collective-permute-start(bf16[64,512]{1,0:T(8,128)(2,1)S(1)} %get-tuple-element.69), channel_id=1, source_target_pairs={{2,0},{4,2},{6,4},{8,6},{10,8},{12,10},{14,12},{16,14},{18,16},{20... | collective-permute-start | bytes 196616 | tf_op jit(solution)/shard_map/ppermute | solution.py:19
  98.1 9.1 %collective-permute-start.10 = (f32[64,1]{1,0:T(8,128)S(1)}, f32[64,1]{1,0:T(8,128)S(1)}, u32[]{:S(2)}, u32[]{:S(2)}) collective-permute-start(f32[64,1]{1,0:T(8,128)S(1)} %get-tuple-element.28), channel_id=1, source_target_pairs={{0,2},{2,4},{4,6},{6,8},{8,10},{10,12},{12,14},{14,16},{16,18},{18... | collective-permute-start | bytes 776 | tf_op jit(solution)/shard_map/ppermute | solution.py:16
  98.1 9.2 %collective-permute-start.11 = (f32[64,1]{1,0:T(8,128)S(1)}, f32[64,1]{1,0:T(8,128)S(1)}, u32[]{:S(2)}, u32[]{:S(2)}) collective-permute-start(f32[64,1]{1,0:T(8,128)S(1)} %get-tuple-element.29), channel_id=1, source_target_pairs={{2,0},{4,2},{6,4},{8,6},{10,8},{12,10},{14,12},{16,14},{18,16},{20... | collective-permute-start | bytes 776 | tf_op jit(solution)/shard_map/ppermute | solution.py:19
  108.0 9.5 %collective-permute-start.12 = (bf16[64,512]{1,0:T(8,128)(2,1)S(1)}, bf16[64,512]{1,0:T(8,128)(2,1)S(1)}, u32[]{:S(2)}, u32[]{:S(2)}) collective-permute-start(bf16[64,512]{1,0:T(8,128)(2,1)S(1)} %get-tuple-element.62), channel_id=1, source_target_pairs={{0,2},{2,4},{4,6},{6,8},{8,10},{10,12},{12,14},{14,16},{16,18},{18... | collective-permute-start | bytes 196616 | tf_op jit(solution)/shard_map/ppermute | solution.py:16
  108.1 9.4 %collective-permute-start.13 = (bf16[64,512]{1,0:T(8,128)(2,1)S(1)}, bf16[64,512]{1,0:T(8,128)(2,1)S(1)}, u32[]{:S(2)}, u32[]{:S(2)}) collective-permute-start(bf16[64,512]{1,0:T(8,128)(2,1)S(1)} %get-tuple-element.63), channel_id=1, source_target_pairs={{2,0},{4,2},{6,4},{8,6},{10,8},{12,10},{14,12},{16,14},{18,16},{20... | collective-permute-start | bytes 196616 | tf_op jit(solution)/shard_map/ppermute | solution.py:19
  130.9 9.1 %collective-permute-start.14 = (f32[64,1]{1,0:T(8,128)S(1)}, f32[64,1]{1,0:T(8,128)S(1)}, u32[]{:S(2)}, u32[]{:S(2)}) collective-permute-start(f32[64,1]{1,0:T(8,128)S(1)} %get-tuple-element.26), channel_id=1, source_target_pairs={{0,2},{2,4},{4,6},{6,8},{8,10},{10,12},{12,14},{14,16},{16,18},{18... | collective-permute-start | bytes 776 | tf_op jit(solution)/shard_map/ppermute | solution.py:16
  131.0 9.6 %collective-permute-start.15 = (f32[64,1]{1,0:T(8,128)S(1)}, f32[64,1]{1,0:T(8,128)S(1)}, u32[]{:S(2)}, u32[]{:S(2)}) collective-permute-start(f32[64,1]{1,0:T(8,128)S(1)} %get-tuple-element.27), channel_id=1, source_target_pairs={{2,0},{4,2},{6,4},{8,6},{10,8},{12,10},{14,12},{16,14},{18,16},{20... | collective-permute-start | bytes 776 | tf_op jit(solution)/shard_map/ppermute | solution.py:19
  190.5 384.3 %reduce-scatter.5.cloned.1.call-start = ((), (), s32[]{:S(2)}) async-start(), calls=%async_computation.7 | async-start | bytes 49152 | tf_op jit(solution)/shard_map/reduce_scatter | solution.py:77
  382.0 9.5 %collective-permute-start.18 = (bf16[64,512]{1,0:T(8,128)(2,1)S(1)}, bf16[64,512]{1,0:T(8,128)(2,1)S(1)}, u32[]{:S(2)}, u32[]{:S(2)}) collective-permute-start(bf16[64,512]{1,0:T(8,128)(2,1)S(1)} %get-tuple-element.56), channel_id=1, source_target_pairs={{0,2},{2,4},{4,6},{6,8},{8,10},{10,12},{12,14},{14,16},{16,18},{18... | collective-permute-start | bytes 196616 | tf_op jit(solution)/shard_map/ppermute | solution.py:16
  382.1 9.5 %collective-permute-start.19 = (bf16[64,512]{1,0:T(8,128)(2,1)S(1)}, bf16[64,512]{1,0:T(8,128)(2,1)S(1)}, u32[]{:S(2)}, u32[]{:S(2)}) collective-permute-start(bf16[64,512]{1,0:T(8,128)(2,1)S(1)} %get-tuple-element.57), channel_id=1, source_target_pairs={{2,0},{4,2},{6,4},{8,6},{10,8},{12,10},{14,12},{16,14},{18,16},{20... | collective-permute-start | bytes 196616 | tf_op jit(solution)/shard_map/ppermute | solution.py:19
  405.1 9.1 %collective-permute-start.20 = (f32[64,1]{1,0:T(8,128)S(1)}, f32[64,1]{1,0:T(8,128)S(1)}, u32[]{:S(2)}, u32[]{:S(2)}) collective-permute-start(f32[64,1]{1,0:T(8,128)S(1)} %get-tuple-element.22), channel_id=1, source_target_pairs={{0,2},{2,4},{4,6},{6,8},{8,10},{10,12},{12,14},{14,16},{16,18},{18... | collective-permute-start | bytes 776 | tf_op jit(solution)/shard_map/ppermute | solution.py:16
  405.1 9.2 %collective-permute-start.21 = (f32[64,1]{1,0:T(8,128)S(1)}, f32[64,1]{1,0:T(8,128)S(1)}, u32[]{:S(2)}, u32[]{:S(2)}) collective-permute-start(f32[64,1]{1,0:T(8,128)S(1)} %get-tuple-element.23), channel_id=1, source_target_pairs={{2,0},{4,2},{6,4},{8,6},{10,8},{12,10},{14,12},{16,14},{18,16},{20... | collective-permute-start | bytes 776 | tf_op jit(solution)/shard_map/ppermute | solution.py:19
  415.0 9.5 %collective-permute-start.22 = (bf16[64,512]{1,0:T(8,128)(2,1)S(1)}, bf16[64,512]{1,0:T(8,128)(2,1)S(1)}, u32[]{:S(2)}, u32[]{:S(2)}) collective-permute-start(bf16[64,512]{1,0:T(8,128)(2,1)S(1)} %get-tuple-element.50), channel_id=1, source_target_pairs={{0,2},{2,4},{4,6},{6,8},{8,10},{10,12},{12,14},{14,16},{16,18},{18... | collective-permute-start | bytes 196616 | tf_op jit(solution)/shard_map/ppermute | solution.py:16
  415.1 9.4 %collective-permute-start.23 = (bf16[64,512]{1,0:T(8,128)(2,1)S(1)}, bf16[64,512]{1,0:T(8,128)(2,1)S(1)}, u32[]{:S(2)}, u32[]{:S(2)}) collective-permute-start(bf16[64,512]{1,0:T(8,128)(2,1)S(1)} %get-tuple-element.51), channel_id=1, source_target_pairs={{2,0},{4,2},{6,4},{8,6},{10,8},{12,10},{14,12},{16,14},{18,16},{20... | collective-permute-start | bytes 196616 | tf_op jit(solution)/shard_map/ppermute | solution.py:19
  440.2 9.2 %collective-permute-start.25 = (f32[64,1]{1,0:T(8,128)S(1)}, f32[64,1]{1,0:T(8,128)S(1)}, u32[]{:S(2)}, u32[]{:S(2)}) collective-permute-start(f32[64,1]{1,0:T(8,128)S(1)} %get-tuple-element.21), channel_id=1, source_target_pairs={{2,0},{4,2},{6,4},{8,6},{10,8},{12,10},{14,12},{16,14},{18,16},{20... | collective-permute-start | bytes 776 | tf_op jit(solution)/shard_map/ppermute | solution.py:19
  450.1 9.5 %collective-permute-start.26 = (bf16[64,512]{1,0:T(8,128)(2,1)S(1)}, bf16[64,512]{1,0:T(8,128)(2,1)S(1)}, u32[]{:S(2)}, u32[]{:S(2)}) collective-permute-start(bf16[64,512]{1,0:T(8,128)(2,1)S(1)} %get-tuple-element.44), channel_id=1, source_target_pairs={{0,2},{2,4},{4,6},{6,8},{8,10},{10,12},{12,14},{14,16},{16,18},{18... | collective-permute-start | bytes 196616 | tf_op jit(solution)/shard_map/ppermute | solution.py:16
  450.2 9.7 %collective-permute-start.27 = (bf16[64,512]{1,0:T(8,128)(2,1)S(1)}, bf16[64,512]{1,0:T(8,128)(2,1)S(1)}, u32[]{:S(2)}, u32[]{:S(2)}) collective-permute-start(bf16[64,512]{1,0:T(8,128)(2,1)S(1)} %get-tuple-element.45), channel_id=1, source_target_pairs={{2,0},{4,2},{6,4},{8,6},{10,8},{12,10},{14,12},{16,14},{18,16},{20... | collective-permute-start | bytes 196616 | tf_op jit(solution)/shard_map/ppermute | solution.py:19
  474.2 9.1 %collective-permute-start.28 = (f32[64,1]{1,0:T(8,128)S(1)}, f32[64,1]{1,0:T(8,128)S(1)}, u32[]{:S(2)}, u32[]{:S(2)}) collective-permute-start(f32[64,1]{1,0:T(8,128)S(1)} %get-tuple-element.18), channel_id=1, source_target_pairs={{0,2},{2,4},{4,6},{6,8},{8,10},{10,12},{12,14},{14,16},{16,18},{18... | collective-permute-start | bytes 776 | tf_op jit(solution)/shard_map/ppermute | solution.py:16
  474.2 9.2 %collective-permute-start.29 = (f32[64,1]{1,0:T(8,128)S(1)}, f32[64,1]{1,0:T(8,128)S(1)}, u32[]{:S(2)}, u32[]{:S(2)}) collective-permute-start(f32[64,1]{1,0:T(8,128)S(1)} %get-tuple-element.19), channel_id=1, source_target_pairs={{2,0},{4,2},{6,4},{8,6},{10,8},{12,10},{14,12},{16,14},{18,16},{20... | collective-permute-start | bytes 776 | tf_op jit(solution)/shard_map/ppermute | solution.py:19
  484.1 9.5 %collective-permute-start.30 = (bf16[64,512]{1,0:T(8,128)(2,1)S(1)}, bf16[64,512]{1,0:T(8,128)(2,1)S(1)}, u32[]{:S(2)}, u32[]{:S(2)}) collective-permute-start(bf16[64,512]{1,0:T(8,128)(2,1)S(1)} %get-tuple-element.38), channel_id=1, source_target_pairs={{0,2},{2,4},{4,6},{6,8},{8,10},{10,12},{12,14},{14,16},{16,18},{18... | collective-permute-start | bytes 196616 | tf_op jit(solution)/shard_map/ppermute | solution.py:16
  484.2 9.4 %collective-permute-start.31 = (bf16[64,512]{1,0:T(8,128)(2,1)S(1)}, bf16[64,512]{1,0:T(8,128)(2,1)S(1)}, u32[]{:S(2)}, u32[]{:S(2)}) collective-permute-start(bf16[64,512]{1,0:T(8,128)(2,1)S(1)} %get-tuple-element.39), channel_id=1, source_target_pairs={{2,0},{4,2},{6,4},{8,6},{10,8},{12,10},{14,12},{16,14},{18,16},{20... | collective-permute-start | bytes 196616 | tf_op jit(solution)/shard_map/ppermute | solution.py:19
  508.6 9.4 %collective-permute-start.33 = (f32[64,1]{1,0:T(8,128)S(1)}, f32[64,1]{1,0:T(8,128)S(1)}, u32[]{:S(2)}, u32[]{:S(2)}) collective-permute-start(f32[64,1]{1,0:T(8,128)S(1)} %get-tuple-element.17), channel_id=1, source_target_pairs={{2,0},{4,2},{6,4},{8,6},{10,8},{12,10},{14,12},{16,14},{18,16},{20... | collective-permute-start | bytes 776 | tf_op jit(solution)/shard_map/ppermute | solution.py:19
  (20 other events, 772.1 us)
Sparse Core Ops, SparseCore 0:
  190.6 7.4 reduce-scatter.2
  567.3 7.4 reduce-scatter.4
